TPU v7x, 32 devices: a whole 2x2x4 slice. The times are simulated.
32 devices in a mesh: groups: 2 (over x), row: 16 (over z, y, core).
Axes of the slice: x: 2, y: 2, z: 4, core: 2. Of those that a mesh axis runs over, the one named last changes fastest.
Arguments:
- pair_rows: bfloat16 [256, 128, 128], P(('groups', 'row')), parts along dimension 0, may hold values from -6 to 6
- in_gain: float32 [128], replicated, may hold values from 0.1 to 1.9
- w_left: bfloat16 [128, 128], replicated, may hold values from -0.5 to 0.5
- w_left_gate: bfloat16 [128, 128], replicated, may hold values from -0.5 to 0.5
- w_right: bfloat16 [128, 128], replicated, may hold values from -0.5 to 0.5
- w_right_gate: bfloat16 [128, 128], replicated, may hold values from -0.5 to 0.5
- w_gate: bfloat16 [128, 128], replicated, may hold values from -0.5 to 0.5
- w_out: bfloat16 [128, 128], replicated, may hold values from -0.5 to 0.5
- out_gain: float32 [128], replicated, may hold values from 0.1 to 1.9
- valid_len: int32 [2], P('groups'), parts along dimension 0, may hold values from 64 to 128
- window: int32 [2], P('groups'), parts along dimension 0, may hold values from 0 to 7
Outputs:
- update: bfloat16 [256, 16, 128], P(('groups', 'row')), parts along dimension 0
There are 2 independent parts, one for each index of `groups`. A program takes and returns all parts, laid end to end along the dimension named above; an argument that names none is the same for every part. Nothing has to cross between parts.
All inputs are finite; a program needn't handle non-finite values.
Results may differ from a plain program's by a relative error of at most 0.0078.
Values may be sent and summed in bfloat16 or wider, within the bound.
A program may use at most 128 MiB of HBM per device.

v0:
```python
import jax
import jax.numpy as jnp
from jax import lax
from jax.sharding import PartitionSpec as P


def layer_norm(values, gain):
    mean_v = jnp.mean(values, axis=-1, keepdims=True)
    centered = values - mean_v
    variance_v = jnp.mean(centered * centered, axis=-1, keepdims=True)
    return centered * lax.rsqrt(variance_v + 1e-05) * gain


def on_device(
    pair_rows,
    in_gain,
    w_left,
    w_left_gate,
    w_right,
    w_right_gate,
    w_gate,
    w_out,
    out_gain,
    valid_len,
    window,
):
    my_index = lax.axis_index("row")
    local_rows, tokens_all, channels = pair_rows.shape
    width_win = tokens_all // 8
    valid_upto = valid_len[0]
    start_block = window[0]
    start_row = start_block * width_win
    row_ids = my_index * local_rows + jnp.arange(local_rows, dtype=jnp.int32)
    row_live = (row_ids < valid_upto).astype(jnp.float32)
    col_live = (jnp.arange(tokens_all, dtype=jnp.int32) < valid_upto).astype(jnp.float32)
    live_mask = (row_live[:, None] * col_live[None, :])[:, :, None]
    normed = layer_norm(pair_rows.astype(jnp.float32), in_gain).astype(jnp.bfloat16)
    flat_rows = normed.reshape(-1, channels)
    joined = jnp.concatenate([w_left, w_left_gate, w_right, w_right_gate], axis=1)
    projected = jnp.dot(flat_rows, joined, preferred_element_type=jnp.float32)
    projected = projected.reshape(local_rows, tokens_all, 4 * channels)
    left_edge = (
        jax.nn.sigmoid(projected[:, :, channels : 2 * channels])
        * projected[:, :, :channels]
        * live_mask
    ).astype(jnp.bfloat16)
    right_edge = (
        jax.nn.sigmoid(projected[:, :, 3 * channels :])
        * projected[:, :, 2 * channels : 3 * channels]
        * live_mask
    ).astype(jnp.bfloat16)
    gate_in = lax.dynamic_slice_in_dim(normed, start_row, width_win, 1)
    gate_vals = jax.nn.sigmoid(
        jnp.dot(gate_in.reshape(-1, channels), w_gate, preferred_element_type=jnp.float32)
    )
    gate_vals = gate_vals.reshape(local_rows, width_win, channels)
    regrouped = lax.all_to_all(right_edge, "row", split_axis=1, concat_axis=0, tiled=True)
    picked = lax.dynamic_slice_in_dim(regrouped, start_row, width_win, 0)
    window_right = lax.all_gather(picked, "row", axis=1, tiled=True)
    product = jnp.einsum(
        "ikc,jkc->ijc", left_edge, window_right, preferred_element_type=jnp.float32
    )
    normed_out = layer_norm(product, out_gain).astype(jnp.bfloat16)
    result = jnp.dot(normed_out.reshape(-1, channels), w_out, preferred_element_type=jnp.float32)
    return (gate_vals * result.reshape(local_rows, width_win, channels)).astype(jnp.bfloat16)


def solution(mesh):
    return jax.shard_map(
        on_device,
        mesh=mesh,
        in_specs=(
            P(("groups", "row"), None, None),
            P(),
            P(),
            P(),
            P(),
            P(),
            P(),
            P(),
            P(),
            P("groups"),
            P("groups"),
        ),
        out_specs=P(("groups", "row"), None, None),
        check_vma=False,
    )
```

profile of v0, /device:TPU:9, one launch (start us, length us, event | category | flops | bytes accessed | tf_op | source)
XLA Modules:
  0.0 75.5 jit_solution(6741622553419118071)
XLA Ops:
  0.0 0.0 copy-start
  0.7 1.1 %convert_reduce_fusion = f32[8,128]{1,0:T(8,128)S(1)} fusion(bf16[8,128,128]{2,1,0:T(8,128)(2,1)} %param.11), kind=kLoop, calls=%fused_computation.7 | loop fusion | flops 261120 | bytes 266240 | tf_op jit(solution)/shard_map/reduce_sum | solution.py:8
  1.8 1.3 %fusion.6 = f32[8,128]{1,0:T(8,128)S(1)} fusion(bf16[8,128,128]{2,1,0:T(8,128)(2,1)} %param.11, f32[8,128]{1,0:T(8,128)S(1)} %broadcast_multiply_fusion.2), kind=kLoop, calls=%fused_computation.10 | loop fusion | flops 523264 | bytes 270336 | tf_op jit(solution)/shard_map/reduce_sum | solution.py:10
  3.1 0.1 broadcast_multiply_fusion.1
  3.2 1.3 %fusion.8 = bf16[8,128,128]{2,1,0:T(8,128)(2,1)S(1)} fusion(bf16[8,128,128]{2,1,0:T(8,128)(2,1)} %param.11, f32[128]{0:T(128)} %param.12, f32[8,128]{1,0:T(8,128)S(1)} %add_rsqrt_fusion.1, f32[8,128]{1,0:T(8,128)S(1)} %broadcast_multiply_fusion.2), kind=kLoop, calls=%fused_computation.12 | loop fusion | flops 655360 | bytes 532992 | tf_op jit(solution)/shard_map/convert_element_type | solution.py:37
  4.5 1.2 %fusion.19 = f32[8,128,512]{2,1,0:T(8,128)S(1)} fusion(bf16[8,128,128]{2,1,0:T(8,128)(2,1)S(1)} %fusion.8, bf16[128,128]{1,0:T(8,128)(2,1)} %param.16, bf16[128,128]{1,0:T(8,128)(2,1)} %param.15, bf16[128,128]{1,0:T(8,128)(2,1)} %param.14, bf16[128,128]{1,0:T(8,128)(2,1)} %param.13), kind=kOutput, calls=%fused_computation.28 | convolution fusion | flops 134742016 | bytes 2490368 | tf_op jit(solution)/shard_map/dot_general | solution.py:40
  5.7 0.3 fusion.10
  6.0 0.9 %copy.29 = bf16[8,128,128]{2,0,1:T(8,128)(2,1)} copy(bf16[8,128,128]{2,1,0:T(8,128)(2,1)S(1)} %get-tuple-element.6) | data formatting | bytes 524288 | tf_op jit(solution)/shard_map/convert_element_type | solution.py:51
  6.9 6.6 %all-to-all-start = ((bf16[8,128,128]{2,0,1:T(8,128)(2,1)}), bf16[8,128,128]{2,0,1:T(8,128)(2,1)S(1)}, u32[]{:S(2)}, u32[]{:S(2)}) async-start(bf16[8,128,128]{2,0,1:T(8,128)(2,1)} %copy.29), calls=%async_computation | async-start | bytes 524288 | tf_op jit(solution)/shard_map/all_to_all | solution.py:57
  14.1 0.2 copy.33
  14.4 0.0 copy-done
  14.4 0.2 fusion.2
  14.5 7.6 %all-to-all-done = bf16[8,128,128]{2,0,1:T(8,128)(2,1)S(1)} async-done(((bf16[8,128,128]{2,0,1:T(8,128)(2,1)}), bf16[8,128,128]{2,0,1:T(8,128)(2,1)S(1)}, u32[]{:S(2)}, u32[]{:S(2)}) %all-to-all-start) | async-done | bytes 262176 | tf_op jit(solution)/shard_map/all_to_all | solution.py:57
  22.2 0.2 copy.36
  22.4 0.0 copy-start.1
  22.5 0.0 copy-start.2
  22.5 50.5 %all_gather.3 = bf16[16,128,128]{0,1,2:T(8,128)(2,1)S(1)} all-gather(bf16[16,8,128]{0,1,2:T(8,128)(2,1)S(1)} %copy.36), channel_id=1, replica_groups=mesh['groups'=2,'row'=16] {'row'}, dimensions={1}, use_global_device_ids=true | all-gather | bytes 557056 | tf_op jit(solution)/shard_map/all_gather | solution.py:59
  73.0 1.2 %fusion.31 = f32[128,16,8]{1,2,0:T(8,128)S(1)} fusion(bf16[16,128,128]{0,1,2:T(8,128)(2,1)S(1)} %all_gather.3, bf16[8,128,128]{1,0,2:T(8,128)(2,1)S(1)} %copy.33), kind=kOutput, calls=%fused_computation.53 | convolution fusion | flops 4194304 | bytes 851968 | tf_op jit(solution)/shard_map/ikc,jkc->ijc/dot_general | solution.py:60
  74.2 0.2 copy.34
  74.4 0.1 bitcast_reduce_fusion
  74.5 0.2 multiply_reduce_fusion
  74.7 0.0 copy-done.1
  74.7 0.0 copy-done.2
  74.7 0.8 %fusion.3 = bf16[8,16,128]{2,1,0:T(8,128)(2,1)} fusion(f32[8,16,128]{2,1,0:T(8,128)S(1)} %bitcast.31, f32[128,16,8]{0,1,2:T(8,128)S(1)} %copy.34, bf16[128,128]{1,0:T(8,128)(2,1)S(1)} %copy-done.1, f32[128]{0:T(128)S(1)} %copy-done.2, f32[8,16]{1,0:T(8,128)S(1)} %add_rsqrt_fusion, f32[8,16]{1,0:T(8,128)S(1)} %broadcast_multiply_fusion), kind=kOutput, calls=%fused_computation.5 | convolution fusion | flops 4292608 | bytes 198144 | tf_op jit(solution)/shard_map/dot_general | solution.py:64
  (9 shorter events, 0.1 us)
Async XLA Ops:
  0.0 14.4 %copy-start = (bf16[128,128]{1,0:T(8,128)(2,1)S(1)}, bf16[128,128]{1,0:T(8,128)(2,1)}, u32[]{:S(2)}) copy-start(bf16[128,128]{1,0:T(8,128)(2,1)} %param.17) | copy-start | bytes 98308
  6.9 15.3 %all-to-all-start = ((bf16[8,128,128]{2,0,1:T(8,128)(2,1)}), bf16[8,128,128]{2,0,1:T(8,128)(2,1)S(1)}, u32[]{:S(2)}, u32[]{:S(2)}) async-start(bf16[8,128,128]{2,0,1:T(8,128)(2,1)} %copy.29), calls=%async_computation | async-start | bytes 524288 | tf_op jit(solution)/shard_map/all_to_all | solution.py:57
  22.4 52.2 %copy-start.1 = (bf16[128,128]{1,0:T(8,128)(2,1)S(1)}, bf16[128,128]{1,0:T(8,128)(2,1)}, u32[]{:S(2)}) copy-start(bf16[128,128]{1,0:T(8,128)(2,1)} %param.18) | copy-start | bytes 98308
  22.5 52.2 %copy-start.2 = (f32[128]{0:T(128)S(1)}, f32[128]{0:T(128)}, u32[]{:S(2)}) copy-start(f32[128]{0:T(128)} %param.19) | copy-start | bytes 1540
where the time goes:
time: 76 us; the launch traced here: 75.5 us
  blocking collectives  50.5 us (66%)
  waiting for transfers between devices  7.63 us (10%)
  starting transfers between devices  6.58 us (9%)
  other arithmetic  4.38 us (6%)
  matrix products  3.4 us (4%)
  local copies, waits for them, and re-layouts  1.53 us (2%)
  between operations  1.5 us (2%)
    all_gather x1, blocking collectives, on_device(): window_right = lax.all_gather(picked, 'row', axis=1, tiled=True)  50.5 us
    all_to_all x1, waiting for transfers between devices, on_device(): lax.all_to_all(right_edge, 'row', split_axis=1, concat_axis=0, tiled=True)  7.63 us
    all_to_all x1, starting transfers between devices, on_device(): lax.all_to_all(right_edge, 'row', split_axis=1, concat_axis=0, tiled=True)  6.58 us
  transfers between devices with their start and end apart: 1, of which 1 were waited for; matrix products, arithmetic and copies ran while one was open for 0% of the time, Pallas kernels for 0%

commit v1 on v0

--- a/solution.py
+++ b/solution.py
@@ -2,6 +2,19 @@
 import jax.numpy as jnp
 from jax import lax
 from jax.sharding import PartitionSpec as P
+
+
+def collect(array, axis, dim):
+    ways = lax.axis_size(axis)
+    up = [(d, (d + 1) % ways) for d in range(ways)]
+    down = [(d, (d - 1) % ways) for d in range(ways)]
+    earlier, later = ([array], [array])
+    for _ in range(ways // 2):
+        earlier.append(lax.ppermute(earlier[-1], axis, up))
+    for _ in range((ways - 1) // 2):
+        later.append(lax.ppermute(later[-1], axis, down))
+    line = jnp.concatenate([*earlier[::-1], *later[1:]], axis=dim)
+    return jnp.roll(line, (lax.axis_index(axis) - ways // 2) * array.shape[dim], axis=dim)
 
 
 def layer_norm(values, gain):
@@ -56,7 +69,7 @@
     gate_vals = gate_vals.reshape(local_rows, width_win, channels)
     regrouped = lax.all_to_all(right_edge, "row", split_axis=1, concat_axis=0, tiled=True)
     picked = lax.dynamic_slice_in_dim(regrouped, start_row, width_win, 0)
-    window_right = lax.all_gather(picked, "row", axis=1, tiled=True)
+    window_right = collect(picked, "row", 1)
     product = jnp.einsum(
         "ikc,jkc->ijc", left_edge, window_right, preferred_element_type=jnp.float32
     )

time: 76 us -> 156 us (2.05); the launches traced: 75.5 us -> 154 us
  waiting for transfers between devices: 7.63 us -> 93.5 us
  blocking collectives: 50.5 us -> 0 us
  local copies, waits for them, and re-layouts: 1.53 us -> 26.6 us
  starting transfers between devices: 6.58 us -> 24.2 us
    ppermute x0 -> x15, waiting for transfers between devices: none -> 85.5 us  [the longest x7 63.9 us: collect(): later.append(lax.ppermute(later[-1], axis, down))]
    all_gather x1 -> x0, blocking collectives: 50.5 us -> none  [on_device(): window_right = lax.all_gather(picked, 'row', axis=1, tiled=True)]
    ppermute x0 -> x15, starting transfers between devices: none -> 17.6 us  [the longest x8 17.6 us: collect(): earlier.append(lax.ppermute(earlier[-1], axis, up))]
    concatenate x0 -> x1, local copies, waits for them, and re-layouts: none -> 15.7 us  [collect(): jnp.roll(line, (lax.axis_index(axis) - ways // 2) * array.shape[dim], axi...]
    all_to_all x1, local copies, waits for them, and re-layouts: 0.04 us -> 7.22 us  [on_device(): lax.all_to_all(right_edge, 'row', split_axis=1, concat_axis=0, tiled=True)]
  transfers between devices with their start and end apart: 1 -> 16, of which waited for: 1 -> 16; matrix products, arithmetic and copies ran while one was open for 0% -> 1% of each run, Pallas kernels for 0% -> 0%
where the time goes in v1:
time: 156 us; the launch traced here: 154 us
  waiting for transfers between devices  93.5 us (60%)
  local copies, waits for them, and re-layouts  26.6 us (17%)
  starting transfers between devices  24.2 us (16%)
  other arithmetic  5.09 us (3%)
  matrix products  2.67 us (2%)
    ppermute x7, waiting for transfers between devices, collect(): later.append(lax.ppermute(later[-1], axis, down))  63.9 us
    ppermute x8, waiting for transfers between devices, collect(): earlier.append(lax.ppermute(earlier[-1], axis, up))  21.6 us
    ppermute x8, starting transfers between devices, collect(): earlier.append(lax.ppermute(earlier[-1], axis, up))  17.6 us
    concatenate x1, local copies, waits for them, and re-layouts, collect(): jnp.roll(line, (lax.axis_index(axis) - ways // 2) * array.shape[dim], axi...  15.7 us
    all_to_all x1, waiting for transfers between devices, on_device(): lax.all_to_all(right_edge, 'row', split_axis=1, concat_axis=0, tiled=True)  8.02 us
    all_to_all x1, local copies, waits for them, and re-layouts, on_device(): lax.all_to_all(right_edge, 'row', split_axis=1, concat_axis=0, tiled=True)  7.22 us
    all_to_all x1, starting transfers between devices, on_device(): lax.all_to_all(right_edge, 'row', split_axis=1, concat_axis=0, tiled=True)  6.58 us
  transfers between devices with their start and end apart: 16, of which 16 were waited for; matrix products, arithmetic and copies ran while one was open for 1% of the time, Pallas kernels for 0%

profile of v1, /device:TPU:9, one launch (start us, length us, event | category | flops | bytes accessed | tf_op | source)
XLA Modules:
  0.0 153.6 jit_solution(5014534823333903058)
XLA Ops:
  0.7 1.1 convert_reduce_fusion
  1.8 1.3 fusion.6
  3.2 1.3 fusion.8
  4.5 1.2 fusion.21
  5.7 1.0 fusion.15
  6.8 0.9 copy.19
  7.6 6.6 %all-to-all-start = ((bf16[8,128,128]{2,0,1:T(8,128)(2,1)}), bf16[8,128,128]{2,0,1:T(8,128)(2,1)S(1)}, u32[]{:S(2)}, u32[]{:S(2)}) async-start(bf16[8,128,128]{2,0,1:T(8,128)(2,1)} %copy.19), calls=%async_computation | async-start | bytes 524288 | tf_op jit(solution)/shard_map/all_to_all | solution.py:70
  14.9 8.0 %all-to-all-done = bf16[8,128,128]{2,0,1:T(8,128)(2,1)S(1)} async-done(((bf16[8,128,128]{2,0,1:T(8,128)(2,1)}), bf16[8,128,128]{2,0,1:T(8,128)(2,1)S(1)}, u32[]{:S(2)}, u32[]{:S(2)}) %all-to-all-start) | async-done | bytes 262176 | tf_op jit(solution)/shard_map/all_to_all | solution.py:70
  22.9 7.2 %copy.20 = bf16[8,16,8,128]{2,0,1,3:T(8,128)(2,1)} copy(bf16[8,16,8,128]{3,0,2,1:T(8,128)(2,1)S(1)} %bitcast.29) | data formatting | bytes 524288 | tf_op jit(solution)/shard_map/all_to_all | solution.py:70
  30.1 1.1 constant_dynamic-slice_fusion
  31.7 11.7 %collective-permute-done = bf16[16,8,128]{1,0,2:T(8,128)(2,1)S(1)} collective-permute-done((bf16[16,8,128]{1,0,2:T(8,128)(2,1)S(1)}, bf16[16,8,128]{1,0,2:T(8,128)(2,1)S(1)}, u32[]{:S(2)}, u32[]{:S(2)}) %collective-permute-start) | collective-permute-done | bytes 32800 | tf_op jit(solution)/shard_map/ppermute | solution.py:13
  43.4 2.5 %collective-permute-start.1 = (bf16[16,8,128]{1,0,2:T(8,128)(2,1)S(1)}, bf16[16,8,128]{1,0,2:T(8,128)(2,1)S(1)}, u32[]{:S(2)}, u32[]{:S(2)}) collective-permute-start(bf16[16,8,128]{1,0,2:T(8,128)(2,1)S(1)} %collective-permute-done), channel_id=1, source_target_pairs={{0,1},{1,2},{2,3},{3,4},{4,5},{5,6},{6,7},{7,8},{8,9},{9,10},{10,1... | collective-permute-start | bytes 98312 | tf_op jit(solution)/shard_map/ppermute | solution.py:13
  45.9 4.7 %collective-permute-done.8 = bf16[16,8,128]{1,0,2:T(8,128)(2,1)S(1)} collective-permute-done((bf16[16,8,128]{1,0,2:T(8,128)(2,1)S(1)}, bf16[16,8,128]{1,0,2:T(8,128)(2,1)S(1)}, u32[]{:S(2)}, u32[]{:S(2)}) %collective-permute-start.8) | collective-permute-done | bytes 32800 | tf_op jit(solution)/shard_map/ppermute | solution.py:15
  50.6 5.7 %collective-permute-done.1 = bf16[16,8,128]{1,0,2:T(8,128)(2,1)S(1)} collective-permute-done((bf16[16,8,128]{1,0,2:T(8,128)(2,1)S(1)}, bf16[16,8,128]{1,0,2:T(8,128)(2,1)S(1)}, u32[]{:S(2)}, u32[]{:S(2)}) %collective-permute-start.1) | collective-permute-done | bytes 32800 | tf_op jit(solution)/shard_map/ppermute | solution.py:13
  56.3 2.5 %collective-permute-start.2 = (bf16[16,8,128]{1,0,2:T(8,128)(2,1)S(1)}, bf16[16,8,128]{1,0,2:T(8,128)(2,1)S(1)}, u32[]{:S(2)}, u32[]{:S(2)}) collective-permute-start(bf16[16,8,128]{1,0,2:T(8,128)(2,1)S(1)} %collective-permute-done.1), channel_id=1, source_target_pairs={{0,1},{1,2},{2,3},{3,4},{4,5},{5,6},{6,7},{7,8},{8,9},{9,10},{10,1... | collective-permute-start | bytes 98312 | tf_op jit(solution)/shard_map/ppermute | solution.py:13
  58.8 11.0 %collective-permute-done.9 = bf16[16,8,128]{1,0,2:T(8,128)(2,1)S(1)} collective-permute-done((bf16[16,8,128]{1,0,2:T(8,128)(2,1)S(1)}, bf16[16,8,128]{1,0,2:T(8,128)(2,1)S(1)}, u32[]{:S(2)}, u32[]{:S(2)}) %collective-permute-start.9) | collective-permute-done | bytes 32800 | tf_op jit(solution)/shard_map/ppermute | solution.py:15
  69.8 0.7 collective-permute-done.2
  70.6 2.4 %collective-permute-start.3 = (bf16[16,8,128]{1,0,2:T(8,128)(2,1)S(1)}, bf16[16,8,128]{1,0,2:T(8,128)(2,1)S(1)}, u32[]{:S(2)}, u32[]{:S(2)}) collective-permute-start(bf16[16,8,128]{1,0,2:T(8,128)(2,1)S(1)} %collective-permute-done.2), channel_id=1, source_target_pairs={{0,1},{1,2},{2,3},{3,4},{4,5},{5,6},{6,7},{7,8},{8,9},{9,10},{10,1... | collective-permute-start | bytes 98312 | tf_op jit(solution)/shard_map/ppermute | solution.py:13
  73.0 11.0 %collective-permute-done.10 = bf16[16,8,128]{1,0,2:T(8,128)(2,1)S(1)} collective-permute-done((bf16[16,8,128]{1,0,2:T(8,128)(2,1)S(1)}, bf16[16,8,128]{1,0,2:T(8,128)(2,1)S(1)}, u32[]{:S(2)}, u32[]{:S(2)}) %collective-permute-start.10) | collective-permute-done | bytes 32800 | tf_op jit(solution)/shard_map/ppermute | solution.py:15
  84.0 0.7 collective-permute-done.3
  84.8 2.4 %collective-permute-start.4 = (bf16[16,8,128]{1,0,2:T(8,128)(2,1)S(1)}, bf16[16,8,128]{1,0,2:T(8,128)(2,1)S(1)}, u32[]{:S(2)}, u32[]{:S(2)}) collective-permute-start(bf16[16,8,128]{1,0,2:T(8,128)(2,1)S(1)} %collective-permute-done.3), channel_id=1, source_target_pairs={{0,1},{1,2},{2,3},{3,4},{4,5},{5,6},{6,7},{7,8},{8,9},{9,10},{10,1... | collective-permute-start | bytes 98312 | tf_op jit(solution)/shard_map/ppermute | solution.py:13
  87.2 11.0 %collective-permute-done.11 = bf16[16,8,128]{1,0,2:T(8,128)(2,1)S(1)} collective-permute-done((bf16[16,8,128]{1,0,2:T(8,128)(2,1)S(1)}, bf16[16,8,128]{1,0,2:T(8,128)(2,1)S(1)}, u32[]{:S(2)}, u32[]{:S(2)}) %collective-permute-start.11) | collective-permute-done | bytes 32800 | tf_op jit(solution)/shard_map/ppermute | solution.py:15
  98.3 0.7 collective-permute-done.4
  99.0 2.4 %collective-permute-start.5 = (bf16[16,8,128]{1,0,2:T(8,128)(2,1)S(1)}, bf16[16,8,128]{1,0,2:T(8,128)(2,1)S(1)}, u32[]{:S(2)}, u32[]{:S(2)}) collective-permute-start(bf16[16,8,128]{1,0,2:T(8,128)(2,1)S(1)} %collective-permute-done.4), channel_id=1, source_target_pairs={{0,1},{1,2},{2,3},{3,4},{4,5},{5,6},{6,7},{7,8},{8,9},{9,10},{10,1... | collective-permute-start | bytes 98312 | tf_op jit(solution)/shard_map/ppermute | solution.py:13
  101.5 11.0 %collective-permute-done.12 = bf16[16,8,128]{1,0,2:T(8,128)(2,1)S(1)} collective-permute-done((bf16[16,8,128]{1,0,2:T(8,128)(2,1)S(1)}, bf16[16,8,128]{1,0,2:T(8,128)(2,1)S(1)}, u32[]{:S(2)}, u32[]{:S(2)}) %collective-permute-start.12) | collective-permute-done | bytes 32800 | tf_op jit(solution)/shard_map/ppermute | solution.py:15
  113.3 2.4 %collective-permute-start.6 = (bf16[16,8,128]{1,0,2:T(8,128)(2,1)S(1)}, bf16[16,8,128]{1,0,2:T(8,128)(2,1)S(1)}, u32[]{:S(2)}, u32[]{:S(2)}) collective-permute-start(bf16[16,8,128]{1,0,2:T(8,128)(2,1)S(1)} %collective-permute-done.5), channel_id=1, source_target_pairs={{0,1},{1,2},{2,3},{3,4},{4,5},{5,6},{6,7},{7,8},{8,9},{9,10},{10,1... | collective-permute-start | bytes 98312 | tf_op jit(solution)/shard_map/ppermute | solution.py:13
  115.7 11.0 %collective-permute-done.13 = bf16[16,8,128]{1,0,2:T(8,128)(2,1)S(1)} collective-permute-done((bf16[16,8,128]{1,0,2:T(8,128)(2,1)S(1)}, bf16[16,8,128]{1,0,2:T(8,128)(2,1)S(1)}, u32[]{:S(2)}, u32[]{:S(2)}) %collective-permute-start.13) | collective-permute-done | bytes 32800 | tf_op jit(solution)/shard_map/ppermute | solution.py:15
  127.4 2.5 %collective-permute-start.7 = (bf16[16,8,128]{1,0,2:T(8,128)(2,1)S(1)}, bf16[16,8,128]{1,0,2:T(8,128)(2,1)}, u32[]{:S(2)}, u32[]{:S(2)}) collective-permute-start(bf16[16,8,128]{1,0,2:T(8,128)(2,1)S(1)} %collective-permute-done.6), channel_id=1, source_target_pairs={{0,1},{1,2},{2,3},{3,4},{4,5},{5,6},{6,7},{7,8},{8,9},{9,10},{10,1... | collective-permute-start | bytes 98312 | tf_op jit(solution)/shard_map/ppermute | solution.py:13
  130.1 1.1 copy.21
  131.3 4.2 %collective-permute-done.14 = bf16[16,8,128]{1,0,2:T(8,128)(2,1)} collective-permute-done((bf16[16,8,128]{1,0,2:T(8,128)(2,1)S(1)}, bf16[16,8,128]{1,0,2:T(8,128)(2,1)}, u32[]{:S(2)}, u32[]{:S(2)}) %collective-permute-start.14) | collective-permute-done | bytes 32800 | tf_op jit(solution)/shard_map/ppermute | solution.py:15
  136.0 15.7 %concatenate.10 = bf16[16,256,128]{1,0,2:T(8,128)(2,1)S(1)} concatenate(bf16[16,8,128]{1,0,2:T(8,128)(2,1)} %collective-permute-done.7, bf16[16,8,128]{1,0,2:T(8,128)(2,1)} %copy-done.10, bf16[16,8,128]{1,0,2:T(8,128)(2,1)} %copy-done.8, bf16[16,8,128]{1,0,2:T(8,128)(2,1)} %copy-done.6, bf16[16,8,128]{1,0,2:T(8,128)(2,1)} %copy-done.4, bf16[16,8,128]{1,0,2:T(8,128)(2,1)} %copy-done.2, ...), dimensions={1} | concatenate | bytes 2097152 | tf_op jit(solution)/shard_map/jit(_roll_dynamic)/concatenate | solution.py:17
  152.8 0.8 fusion.3
  (50 shorter events, 4.1 us)
Async XLA Ops:
  0.0 129.9 %copy-start = (bf16[128,128]{1,0:T(8,128)(2,1)S(1)}, bf16[128,128]{1,0:T(8,128)(2,1)}, u32[]{:S(2)}) copy-start(bf16[128,128]{1,0:T(8,128)(2,1)} %param.17) | copy-start | bytes 98308
  7.6 15.3 %all-to-all-start = ((bf16[8,128,128]{2,0,1:T(8,128)(2,1)}), bf16[8,128,128]{2,0,1:T(8,128)(2,1)S(1)}, u32[]{:S(2)}, u32[]{:S(2)}) async-start(bf16[8,128,128]{2,0,1:T(8,128)(2,1)} %copy.19), calls=%async_computation | async-start | bytes 524288 | tf_op jit(solution)/shard_map/all_to_all | solution.py:70
  31.2 12.3 %collective-permute-start = (bf16[16,8,128]{1,0,2:T(8,128)(2,1)S(1)}, bf16[16,8,128]{1,0,2:T(8,128)(2,1)S(1)}, u32[]{:S(2)}, u32[]{:S(2)}) collective-permute-start(bf16[16,8,128]{1,0,2:T(8,128)(2,1)S(1)} %constant_dynamic-slice_fusion), channel_id=1, source_target_pairs={{0,1},{1,2},{2,3},{3,4},{4,5},{5,6},{6,7},{7,8},{8,9},{9,10},{10,1... | collective-permute-start | bytes 98312 | tf_op jit(solution)/shard_map/ppermute | solution.py:13
  31.7 18.9 %collective-permute-start.8 = (bf16[16,8,128]{1,0,2:T(8,128)(2,1)S(1)}, bf16[16,8,128]{1,0,2:T(8,128)(2,1)S(1)}, u32[]{:S(2)}, u32[]{:S(2)}) collective-permute-start(bf16[16,8,128]{1,0,2:T(8,128)(2,1)S(1)} %constant_dynamic-slice_fusion), channel_id=1, source_target_pairs={{0,15},{1,0},{2,1},{3,2},{4,3},{5,4},{6,5},{7,6},{8,7},{9,8},{10,9... | collective-permute-start | bytes 98312 | tf_op jit(solution)/shard_map/ppermute | solution.py:15
  43.4 12.8 %collective-permute-start.1 = (bf16[16,8,128]{1,0,2:T(8,128)(2,1)S(1)}, bf16[16,8,128]{1,0,2:T(8,128)(2,1)S(1)}, u32[]{:S(2)}, u32[]{:S(2)}) collective-permute-start(bf16[16,8,128]{1,0,2:T(8,128)(2,1)S(1)} %collective-permute-done), channel_id=1, source_target_pairs={{0,1},{1,2},{2,3},{3,4},{4,5},{5,6},{6,7},{7,8},{8,9},{9,10},{10,1... | collective-permute-start | bytes 98312 | tf_op jit(solution)/shard_map/ppermute | solution.py:13
  50.6 19.2 %collective-permute-start.9 = (bf16[16,8,128]{1,0,2:T(8,128)(2,1)S(1)}, bf16[16,8,128]{1,0,2:T(8,128)(2,1)S(1)}, u32[]{:S(2)}, u32[]{:S(2)}) collective-permute-start(bf16[16,8,128]{1,0,2:T(8,128)(2,1)S(1)} %collective-permute-done.8), channel_id=1, source_target_pairs={{0,15},{1,0},{2,1},{3,2},{4,3},{5,4},{6,5},{7,6},{8,7},{9,8},{10,9... | collective-permute-start | bytes 98312 | tf_op jit(solution)/shard_map/ppermute | solution.py:15
  56.3 14.2 %collective-permute-start.2 = (bf16[16,8,128]{1,0,2:T(8,128)(2,1)S(1)}, bf16[16,8,128]{1,0,2:T(8,128)(2,1)S(1)}, u32[]{:S(2)}, u32[]{:S(2)}) collective-permute-start(bf16[16,8,128]{1,0,2:T(8,128)(2,1)S(1)} %collective-permute-done.1), channel_id=1, source_target_pairs={{0,1},{1,2},{2,3},{3,4},{4,5},{5,6},{6,7},{7,8},{8,9},{9,10},{10,1... | collective-permute-start | bytes 98312 | tf_op jit(solution)/shard_map/ppermute | solution.py:13
  69.8 0.8 copy-start.1
  69.8 14.2 %collective-permute-start.10 = (bf16[16,8,128]{1,0,2:T(8,128)(2,1)S(1)}, bf16[16,8,128]{1,0,2:T(8,128)(2,1)S(1)}, u32[]{:S(2)}, u32[]{:S(2)}) collective-permute-start(bf16[16,8,128]{1,0,2:T(8,128)(2,1)S(1)} %collective-permute-done.9), channel_id=1, source_target_pairs={{0,15},{1,0},{2,1},{3,2},{4,3},{5,4},{6,5},{7,6},{8,7},{9,8},{10,9... | collective-permute-start | bytes 98312 | tf_op jit(solution)/shard_map/ppermute | solution.py:15
  70.6 13.4 %copy-start.2 = (bf16[16,8,128]{1,0,2:T(8,128)(2,1)}, bf16[16,8,128]{1,0,2:T(8,128)(2,1)S(1)}, u32[]{:S(2)}) copy-start(bf16[16,8,128]{1,0,2:T(8,128)(2,1)S(1)} %collective-permute-done.2) | copy-start | bytes 98308
  70.6 14.2 %collective-permute-start.3 = (bf16[16,8,128]{1,0,2:T(8,128)(2,1)S(1)}, bf16[16,8,128]{1,0,2:T(8,128)(2,1)S(1)}, u32[]{:S(2)}, u32[]{:S(2)}) collective-permute-start(bf16[16,8,128]{1,0,2:T(8,128)(2,1)S(1)} %collective-permute-done.2), channel_id=1, source_target_pairs={{0,1},{1,2},{2,3},{3,4},{4,5},{5,6},{6,7},{7,8},{8,9},{9,10},{10,1... | collective-permute-start | bytes 98312 | tf_op jit(solution)/shard_map/ppermute | solution.py:13
  84.0 0.8 copy-start.3
  84.0 14.2 %collective-permute-start.11 = (bf16[16,8,128]{1,0,2:T(8,128)(2,1)S(1)}, bf16[16,8,128]{1,0,2:T(8,128)(2,1)S(1)}, u32[]{:S(2)}, u32[]{:S(2)}) collective-permute-start(bf16[16,8,128]{1,0,2:T(8,128)(2,1)S(1)} %collective-permute-done.10), channel_id=1, source_target_pairs={{0,15},{1,0},{2,1},{3,2},{4,3},{5,4},{6,5},{7,6},{8,7},{9,8},{10,9... | collective-permute-start | bytes 98312 | tf_op jit(solution)/shard_map/ppermute | solution.py:15
  84.8 13.4 %copy-start.4 = (bf16[16,8,128]{1,0,2:T(8,128)(2,1)}, bf16[16,8,128]{1,0,2:T(8,128)(2,1)S(1)}, u32[]{:S(2)}) copy-start(bf16[16,8,128]{1,0,2:T(8,128)(2,1)S(1)} %collective-permute-done.3) | copy-start | bytes 98308
  84.8 14.2 %collective-permute-start.4 = (bf16[16,8,128]{1,0,2:T(8,128)(2,1)S(1)}, bf16[16,8,128]{1,0,2:T(8,128)(2,1)S(1)}, u32[]{:S(2)}, u32[]{:S(2)}) collective-permute-start(bf16[16,8,128]{1,0,2:T(8,128)(2,1)S(1)} %collective-permute-done.3), channel_id=1, source_target_pairs={{0,1},{1,2},{2,3},{3,4},{4,5},{5,6},{6,7},{7,8},{8,9},{9,10},{10,1... | collective-permute-start | bytes 98312 | tf_op jit(solution)/shard_map/ppermute | solution.py:13
  98.2 0.8 copy-start.5
  98.2 14.2 %collective-permute-start.12 = (bf16[16,8,128]{1,0,2:T(8,128)(2,1)S(1)}, bf16[16,8,128]{1,0,2:T(8,128)(2,1)S(1)}, u32[]{:S(2)}, u32[]{:S(2)}) collective-permute-start(bf16[16,8,128]{1,0,2:T(8,128)(2,1)S(1)} %collective-permute-done.11), channel_id=1, source_target_pairs={{0,15},{1,0},{2,1},{3,2},{4,3},{5,4},{6,5},{7,6},{8,7},{9,8},{10,9... | collective-permute-start | bytes 98312 | tf_op jit(solution)/shard_map/ppermute | solution.py:15
  99.0 13.4 %copy-start.6 = (bf16[16,8,128]{1,0,2:T(8,128)(2,1)}, bf16[16,8,128]{1,0,2:T(8,128)(2,1)S(1)}, u32[]{:S(2)}) copy-start(bf16[16,8,128]{1,0,2:T(8,128)(2,1)S(1)} %collective-permute-done.4) | copy-start | bytes 98308
  99.0 14.2 %collective-permute-start.5 = (bf16[16,8,128]{1,0,2:T(8,128)(2,1)S(1)}, bf16[16,8,128]{1,0,2:T(8,128)(2,1)S(1)}, u32[]{:S(2)}, u32[]{:S(2)}) collective-permute-start(bf16[16,8,128]{1,0,2:T(8,128)(2,1)S(1)} %collective-permute-done.4), channel_id=1, source_target_pairs={{0,1},{1,2},{2,3},{3,4},{4,5},{5,6},{6,7},{7,8},{8,9},{9,10},{10,1... | collective-permute-start | bytes 98312 | tf_op jit(solution)/shard_map/ppermute | solution.py:13
  112.5 0.8 copy-start.7
  112.5 14.2 %collective-permute-start.13 = (bf16[16,8,128]{1,0,2:T(8,128)(2,1)S(1)}, bf16[16,8,128]{1,0,2:T(8,128)(2,1)S(1)}, u32[]{:S(2)}, u32[]{:S(2)}) collective-permute-start(bf16[16,8,128]{1,0,2:T(8,128)(2,1)S(1)} %collective-permute-done.12), channel_id=1, source_target_pairs={{0,15},{1,0},{2,1},{3,2},{4,3},{5,4},{6,5},{7,6},{8,7},{9,8},{10,9... | collective-permute-start | bytes 98312 | tf_op jit(solution)/shard_map/ppermute | solution.py:15
  113.3 13.4 %copy-start.8 = (bf16[16,8,128]{1,0,2:T(8,128)(2,1)}, bf16[16,8,128]{1,0,2:T(8,128)(2,1)S(1)}, u32[]{:S(2)}) copy-start(bf16[16,8,128]{1,0,2:T(8,128)(2,1)S(1)} %collective-permute-done.5) | copy-start | bytes 98308
  113.3 14.1 %collective-permute-start.6 = (bf16[16,8,128]{1,0,2:T(8,128)(2,1)S(1)}, bf16[16,8,128]{1,0,2:T(8,128)(2,1)S(1)}, u32[]{:S(2)}, u32[]{:S(2)}) collective-permute-start(bf16[16,8,128]{1,0,2:T(8,128)(2,1)S(1)} %collective-permute-done.5), channel_id=1, source_target_pairs={{0,1},{1,2},{2,3},{3,4},{4,5},{5,6},{6,7},{7,8},{8,9},{9,10},{10,1... | collective-permute-start | bytes 98312 | tf_op jit(solution)/shard_map/ppermute | solution.py:13
  126.7 8.7 %copy-start.9 = (bf16[16,8,128]{1,0,2:T(8,128)(2,1)}, bf16[16,8,128]{1,0,2:T(8,128)(2,1)S(1)}, u32[]{:S(2)}) copy-start(bf16[16,8,128]{1,0,2:T(8,128)(2,1)S(1)} %collective-permute-done.13) | copy-start | bytes 98308
  126.7 8.7 %collective-permute-start.14 = (bf16[16,8,128]{1,0,2:T(8,128)(2,1)S(1)}, bf16[16,8,128]{1,0,2:T(8,128)(2,1)}, u32[]{:S(2)}, u32[]{:S(2)}) collective-permute-start(bf16[16,8,128]{1,0,2:T(8,128)(2,1)S(1)} %collective-permute-done.13), channel_id=1, source_target_pairs={{0,15},{1,0},{2,1},{3,2},{4,3},{5,4},{6,5},{7,6},{8,7},{9,8},{10,9... | collective-permute-start | bytes 98312 | tf_op jit(solution)/shard_map/ppermute | solution.py:15
  127.4 8.0 %copy-start.10 = (bf16[16,8,128]{1,0,2:T(8,128)(2,1)}, bf16[16,8,128]{1,0,2:T(8,128)(2,1)S(1)}, u32[]{:S(2)}) copy-start(bf16[16,8,128]{1,0,2:T(8,128)(2,1)S(1)} %collective-permute-done.6) | copy-start | bytes 98308
  127.4 8.6 %collective-permute-start.7 = (bf16[16,8,128]{1,0,2:T(8,128)(2,1)S(1)}, bf16[16,8,128]{1,0,2:T(8,128)(2,1)}, u32[]{:S(2)}, u32[]{:S(2)}) collective-permute-start(bf16[16,8,128]{1,0,2:T(8,128)(2,1)S(1)} %collective-permute-done.6), channel_id=1, source_target_pairs={{0,1},{1,2},{2,3},{3,4},{4,5},{5,6},{6,7},{7,8},{8,9},{9,10},{10,1... | collective-permute-start | bytes 98312 | tf_op jit(solution)/shard_map/ppermute | solution.py:13
  131.2 21.5 %copy-start.11 = (bf16[128,128]{1,0:T(8,128)(2,1)S(1)}, bf16[128,128]{1,0:T(8,128)(2,1)}, u32[]{:S(2)}) copy-start(bf16[128,128]{1,0:T(8,128)(2,1)} %param.18) | copy-start | bytes 98308
  131.3 21.5 %copy-start.12 = (f32[128]{0:T(128)S(1)}, f32[128]{0:T(128)}, u32[]{:S(2)}) copy-start(f32[128]{0:T(128)} %param.19) | copy-start | bytes 1540
